TPU v7x, 256 devices: a whole 4x4x8 slice. The times are simulated.
256 devices in a mesh: req: 16 (over y_hi, x, core), tp: 16 (over y_lo, z).
Axes of the slice: x: 4, y: 4 (y_hi: 2, y_lo: 2; y = y_hi * 2 + y_lo), z: 8, core: 2. Of those that a mesh axis runs over, the one named last changes fastest.
Arguments:
- tokens: bfloat16 [14336, 5120], P(('req', 'tp')), may hold values from -6 to 6
- qkv_weight: bfloat16 [5120, 3, 4096], P('req', None, 'tp')
- out_weight: bfloat16 [4096, 5120], P('tp', 'req')
- query_key_gain: float32 [2, 4096], P(None, 'tp'), may hold values from 0.25 to 1.75
- post_gain: float32 [5120], replicated, may hold values from 0.25 to 1.75
- pool_cache: bfloat16 [512, 128, 2, 4096], P('req', None, None, 'tp'), may hold values from -68 to 68
- lengths: int32 [16, 16], P('req'), may hold values from 1 to 256, 896 in all within a row
- prefix_pages: int32 [16, 16], P('req'), may hold values from 1 to 16, 32 in all within a row
- pool_order: int32 [16, 32], P('req'), may hold values from 0 to 31, each once within a row
- owners: int32 [16, 16], P('req'), may hold values from 0 to 15, each once within a row
Outputs:
- hidden: bfloat16 [14336, 5120], P(('req', 'tp'))
- handed_pages: bfloat16 [512, 128, 2, 4096], P('req', None, None, 'tp')
Inputs may be any that keep to these rules, and one draw needn't show every extreme that they name: `lengths`: each row sums to 896; the largest entry of every row is exactly 256. `prefix_pages`: each row sums to 32; the largest entry of every row is exactly 16. `pool_order`: each row names every slot once. `owners`: each row names every owner once.
All inputs are finite; a program needn't handle non-finite values.
Results may differ from a plain program's by a relative error of at most 0.014.
Values may be sent and summed in bfloat16 or wider, within the bound.
A program may use at most 128 MiB of HBM per device.

v0:
```python
import jax
import jax.numpy as jnp
from jax import lax
from jax.sharding import PartitionSpec as P

HEADS = 32
HEAD = 128
PAGE = 128
CAP = 2
norm_eps = 1e-06
rope_base = 500000.0
masked_score = -1e30


def token_layout(lengths_row, prefix_row, block_len):
    ends_at = jnp.cumsum(lengths_row)
    starts_at = ends_at - lengths_row
    token_ids = jnp.arange(block_len, dtype=jnp.int32)
    request_of = jnp.sum((token_ids[:, None] >= ends_at[None, :]).astype(jnp.int32), axis=1)
    one_hot = (
        request_of[:, None] == jnp.arange(lengths_row.shape[0], dtype=jnp.int32)[None, :]
    ).astype(jnp.int32)
    shift_of = jnp.sum(one_hot * (prefix_row * PAGE - starts_at)[None, :], axis=1)
    return (request_of, token_ids + shift_of, starts_at)


def slot_owner(prefix_row, order_row):
    page_ends = jnp.cumsum(prefix_row)
    page_ids = jnp.arange(order_row.shape[0], dtype=jnp.int32)
    page_request = jnp.sum((page_ids[:, None] >= page_ends[None, :]).astype(jnp.int32), axis=1)
    matches = (order_row[None, :] == page_ids[:, None]).astype(jnp.int32)
    return jnp.sum(matches * page_request[None, :], axis=1)


def rotate_heads(tensor, positions):
    half_dim = HEAD // 2
    frequency = rope_base ** (-(2.0 * jnp.arange(half_dim, dtype=jnp.float32)) / HEAD)
    angles = positions.astype(jnp.float32)[:, None] * frequency[None, :]
    cosine = jnp.cos(angles)[:, None, :]
    sine_part = jnp.sin(angles)[:, None, :]
    first_half = tensor[..., :half_dim]
    second_half = tensor[..., half_dim:]
    return jnp.concatenate(
        [
            first_half * cosine - second_half * sine_part,
            second_half * cosine + first_half * sine_part,
        ],
        axis=-1,
    )


def attend_head(queries, pool_keys, pool_values, new_keys, new_values, pool_mask, block_mask):
    score_scale = HEAD ** (-0.5)
    pool_scores = jnp.dot(queries, pool_keys.T, preferred_element_type=jnp.float32) * score_scale
    block_scores = jnp.dot(queries, new_keys.T, preferred_element_type=jnp.float32) * score_scale
    pool_scores = jnp.where(pool_mask, pool_scores, masked_score)
    block_scores = jnp.where(block_mask, block_scores, masked_score)
    row_max = jnp.maximum(jnp.max(pool_scores, axis=1), jnp.max(block_scores, axis=1))
    pool_exp = jnp.exp(pool_scores - row_max[:, None])
    block_exp = jnp.exp(block_scores - row_max[:, None])
    row_total = jnp.sum(pool_exp, axis=1) + jnp.sum(block_exp, axis=1)
    pool_weights = (pool_exp / row_total[:, None]).astype(jnp.bfloat16)
    block_weights = (block_exp / row_total[:, None]).astype(jnp.bfloat16)
    mixed_out = jnp.dot(pool_weights, pool_values, preferred_element_type=jnp.float32)
    mixed_out = mixed_out + jnp.dot(block_weights, new_values, preferred_element_type=jnp.float32)
    return mixed_out.astype(jnp.bfloat16)


def build_send(kv_new, lengths_row, starts_at, owner_row):
    page_span = CAP * PAGE
    owner_count = owner_row.shape[0]
    owner_ids = jnp.arange(owner_count, dtype=jnp.int32)
    owner_pick = (owner_row[None, :] == owner_ids[:, None]).astype(jnp.int32)
    start_of = jnp.sum(owner_pick * starts_at[None, :], axis=1)
    length_of = jnp.sum(owner_pick * lengths_row[None, :], axis=1)
    offsets = jnp.arange(page_span, dtype=jnp.int32)
    source = start_of[:, None] + offsets[None, :]
    is_valid = offsets[None, :] < length_of[:, None]
    source = jnp.clip(source, 0, kv_new.shape[0] - 1).reshape(-1)
    taken_rows = jnp.take(kv_new, source, axis=0).reshape(
        owner_count, page_span, kv_new.shape[1], kv_new.shape[2]
    )
    return jnp.where(is_valid[:, :, None, None], taken_rows, jnp.zeros_like(taken_rows))


def hand_over(kv_new, lengths_row, starts_at, owner_row):
    outgoing = build_send(kv_new, lengths_row, starts_at, owner_row)
    arrived = lax.all_to_all(outgoing, "req", split_axis=0, concat_axis=0, tiled=True)
    return arrived.reshape(arrived.shape[0] * CAP, PAGE, arrived.shape[2], arrived.shape[3])


def body(
    tokens,
    qkv_weight,
    out_weight,
    query_key_gain,
    post_gain,
    pool_cache,
    lengths,
    prefix_pages,
    pool_order,
    owners,
):
    local_width = qkv_weight.shape[2]
    heads_here = local_width // HEAD
    block_tokens = lax.all_gather(tokens, "tp", axis=0, tiled=True)
    block_len = block_tokens.shape[0]
    row_piece = lax.all_gather(qkv_weight, "req", axis=0, tiled=True)
    flat_piece = row_piece.reshape(row_piece.shape[0], 3 * local_width)
    joined_all = jnp.dot(block_tokens, flat_piece, preferred_element_type=jnp.float32)
    joined_all = joined_all.reshape(block_len, 3, local_width)
    queries = joined_all[:, 0]
    keys_raw = joined_all[:, 1]
    values_raw = joined_all[:, 2]
    local_sums = jnp.stack(
        [jnp.sum(queries * queries, axis=1), jnp.sum(keys_raw * keys_raw, axis=1)]
    )
    global_sums = lax.psum(local_sums, "tp")
    inverse = lax.rsqrt(global_sums / (HEADS * HEAD) + norm_eps)
    queries = queries * inverse[0][:, None] * query_key_gain[0]
    keys_raw = keys_raw * inverse[1][:, None] * query_key_gain[1]
    lengths_row = lengths[0]
    prefix_row = prefix_pages[0]
    request_of, positions, starts_at = token_layout(lengths_row, prefix_row, block_len)
    query_rot = rotate_heads(queries.reshape(block_len, heads_here, HEAD), positions).astype(
        jnp.bfloat16
    )
    key_rot = rotate_heads(keys_raw.reshape(block_len, heads_here, HEAD), positions).astype(
        jnp.bfloat16
    )
    value_new = values_raw.reshape(block_len, heads_here, HEAD).astype(jnp.bfloat16)
    kv_new = jnp.stack(
        [key_rot.reshape(block_len, local_width), value_new.reshape(block_len, local_width)], axis=1
    )
    pool_count = pool_cache.shape[0]
    key_owner = jnp.repeat(slot_owner(prefix_row, pool_order[0]), PAGE)
    pool_mask = request_of[:, None] == key_owner[None, :]
    token_ids = jnp.arange(block_len, dtype=jnp.int32)
    block_mask = (request_of[:, None] == request_of[None, :]) & (
        token_ids[None, :] <= token_ids[:, None]
    )
    pool_keys = pool_cache[:, :, 0, :].reshape(pool_count * PAGE, heads_here, HEAD)
    pool_values = pool_cache[:, :, 1, :].reshape(pool_count * PAGE, heads_here, HEAD)
    head_outs = lax.map(
        lambda per_head: attend_head(
            per_head[0], per_head[1], per_head[2], per_head[3], per_head[4], pool_mask, block_mask
        ),
        (
            jnp.moveaxis(query_rot, 1, 0),
            jnp.moveaxis(pool_keys, 1, 0),
            jnp.moveaxis(pool_values, 1, 0),
            jnp.moveaxis(key_rot, 1, 0),
            jnp.moveaxis(value_new, 1, 0),
        ),
    )
    attention = jnp.moveaxis(head_outs, 0, 1).reshape(block_len, local_width)
    out_full = lax.all_gather(out_weight, "req", axis=1, tiled=True)
    projected = lax.psum_scatter(
        jnp.dot(attention, out_full, preferred_element_type=jnp.float32).astype(jnp.bfloat16),
        "tp",
        scatter_dimension=0,
        tiled=True,
    ).astype(jnp.float32)
    post_scale = lax.rsqrt(jnp.mean(projected * projected, axis=1, keepdims=True) + norm_eps)
    hidden = (tokens.astype(jnp.float32) + projected * post_scale * post_gain[None, :]).astype(
        jnp.bfloat16
    )
    handed_pages = hand_over(kv_new, lengths_row, starts_at, owners[0])
    return (hidden, handed_pages)


def solution(mesh):
    in_specs = (
        P(("req", "tp"), None),
        P("req", None, "tp"),
        P("tp", "req"),
        P(None, "tp"),
        P(),
        P("req", None, None, "tp"),
        P("req", None),
        P("req", None),
        P("req", None),
        P("req", None),
    )
    out_specs = (P(("req", "tp"), None), P("req", None, None, "tp"))
    return jax.shard_map(body, mesh=mesh, in_specs=in_specs, out_specs=out_specs, check_vma=False)
```

profile of v0, /device:TPU:1, one launch (start us, length us, event | category | flops | bytes accessed | tf_op | source)
XLA Modules:
  0.0 490.8 jit_solution(5319571095638446805)
XLA Ops:
  7.2 0.7 all-gather.6.cloned.1.call-update
  7.9 0.7 all-gather.4.cloned.1.call-update
  8.7 0.7 all-gather.8.cloned.1.call-update
  9.5 0.8 fusion.45
  10.2 0.7 copy.47
  11.0 0.1 reduce.3
  11.1 0.1 convert_reduce_fusion
  11.2 1.2 fusion.43
  12.5 21.7 %slice_reduce_fusion = (bf16[32,128,256]{2,1,0:T(8,128)(2,1)}, bf16[32,128,256]{2,1,0:T(8,128)(2,1)}) fusion(bf16[32,128,2,256]{3,2,1,0:T(2,128)(2,1)} %param.17), kind=kLoop, calls=%fused_computation.45 | loop fusion | bytes 8388608 | tf_op jit(solution)/shard_map/slice | solution.py:143
  34.2 2.6 reshape.260
  36.8 4.0 reshape.259
  40.7 0.1 copy.52
  40.8 0.1 reduce.8
  41.0 0.1 convert_reduce_fusion.1
  41.1 0.1 select_reduce_fusion.1
  41.3 1.7 multiply_cosine_fusion
  42.9 4.2 copy_bitcast_fusion
  47.1 43.6 %all-gather.6.cloned.1.call-done = bf16[5120,3,256]{2,0,1:T(8,128)(2,1)} async-done(((bf16[320,3,256]{2,0,1:T(8,128)(2,1)}), bf16[5120,3,256]{2,0,1:T(8,128)(2,1)}) %all-gather.6.cloned.1.call-update) | async-done | bytes 7864336 | tf_op jit(solution)/shard_map/all_gather | solution.py:108
  90.7 10.8 %copy.45 = bf16[5120,3,256]{0,2,1:T(8,128)(2,1)} copy(bf16[5120,3,256]{2,0,1:T(8,128)(2,1)} %all-gather.6.cloned.1.call-done) | data formatting | bytes 15728640 | tf_op jit(solution)/shard_map/all_gather | solution.py:108
  101.5 97.4 %all-gather.4.cloned.1.call-done = bf16[896,5120]{1,0:T(8,128)(2,1)} async-done(((bf16[56,5120]{1,0:T(8,128)(2,1)}), bf16[896,5120]{1,0:T(8,128)(2,1)}) %all-gather.4.cloned.1.call-update) | async-done | bytes 9175056 | tf_op jit(solution)/shard_map/all_gather | solution.py:106
  198.9 12.0 %fusion.32 = f32[896,3,256]{0,2,1:T(8,128)S(1)} fusion(bf16[896,5120]{1,0:T(8,128)(2,1)} %all-gather.4.cloned.1.call-done, bf16[5120,3,256]{0,2,1:T(8,128)(2,1)} %copy.45), kind=kOutput, calls=%fused_computation.39 | convolution fusion | flops 7046430720 | bytes 19791872 | tf_op jit(solution)/shard_map/dot_general | solution.py:110
  210.9 1.1 multiply_reduce_fusion.1
  212.1 2.6 copy.49
  214.7 26.0 %psum.7 = f32[2,896]{1,0:T(2,128)S(1)} all-reduce(f32[2,896]{1,0:T(2,128)S(1)} %pad_maximum_fusion.1), channel_id=1, replica_groups=mesh['req'=16,'tp'=16] {'tp'}, use_global_device_ids=true, to_apply=%region_2.0 | all-reduce | flops 1792 | bytes 14336 | tf_op jit(solution)/shard_map/psum | solution.py:118
  240.8 1.2 copy.46
  242.0 1.8 multiply_multiply_fusion
  243.8 0.4 subtract_convert_fusion
  244.2 0.4 multiply_subtract_fusion
  244.7 0.3 copy.51
  244.9 1.0 maximum_bitcast_fusion
  246.0 0.3 fusion.48
  246.2 59.5 %while.12 = (s32[]{:T(128)}, bf16[2,896,128]{1,2,0:T(8,128)(2,1)}, bf16[2,896,128]{2,1,0:T(8,128)(2,1)}, bf16[2,4096,128]{2,1,0:T(8,128)(2,1)}, bf16[2,896,128]{...) while((s32[]{:T(128)}, bf16[2,896,128]{1,2,0:T(8,128)(2,1)}, ...), condition=%wide.region_14.15_spmd.clone.clone, body=%wide.region_9.14_spmd.clone.clone.sunk | while | flops 2354198784 | bytes 70941888 | solution.py:144
  246.3 9.3 %fusion.59 = (f32[896]{0:T(1024)S(1)}, f32[896,4096]{1,0:T(8,128)}) fusion(s32[4096]{0:T(1024)S(1)} %get-tuple-element.264, s32[896]{0:T(1024)S(1)} %get-tuple-element.265, bf16[2,4096,128]{2,1,0:T(8,128)(2,1)} %get-tuple-element.260, s32[]{:T(128)S(6)} %copy.72, bf16[2,896,128]{2,1,0:T(8,128)(2,1)} %get-tuple-element.259), kind=kOutput, calls=%fused_computation.7.clone.1 | convolution fusion | flops 954203264 | bytes 15982592 | tf_op jit(solution)/shard_map/while/body/eval_jaxpr/dot_general | solution.py:54
  255.5 1.6 fusion.60
  257.2 8.8 %fusion.61 = f32[896]{0:T(1024)S(1)} fusion(f32[896,4096]{1,0:T(8,128)} %get-tuple-element.233, s32[4096]{0:T(1024)S(1)} %get-tuple-element.264, f32[896]{0:T(1024)S(1)} %max.23, s32[896]{0:T(1024)S(1)} %get-tuple-element.265), kind=kLoop, calls=%fused_computation.6.clone.1 | loop fusion | flops 18349184 | bytes 14707200 | tf_op jit(solution)/shard_map/while/body/eval_jaxpr/reduce_sum | solution.py:61
  266.0 0.5 fusion.62
  266.5 7.7 %fusion.63 = f32[896,128]{1,0:T(8,128)S(1)} fusion(f32[896,4096]{1,0:T(8,128)} %get-tuple-element.233, s32[4096]{0:T(1024)S(1)} %get-tuple-element.264, f32[896]{0:T(1024)S(1)} %add.169, f32[896]{0:T(1024)S(1)} %max.23, s32[896]{0:T(1024)S(1)} %get-tuple-element.265, bf16[2,4096,128]{2,1,0:T(8,128)(2,1)S(1)} %copy-done.7, s32[]{:T(128)S(6)} %copy.72), kind=kOutput, calls=%fused_computation.8.clone.1 | convolution fusion | flops 961544192 | bytes 16216068 | tf_op jit(solution)/shard_map/while/body/eval_jaxpr/dot_general | solution.py:64
  274.2 0.7 fusion.64
  274.9 0.2 copy.68
  275.1 0.1 copy-done.8
  275.3 0.8 copy-done.9
  276.0 9.2 %fusion.59 = (f32[896]{0:T(1024)S(1)}, f32[896,4096]{1,0:T(8,128)}) fusion(s32[4096]{0:T(1024)S(1)} %get-tuple-element.264, s32[896]{0:T(1024)S(1)} %get-tuple-element.265, bf16[2,4096,128]{2,1,0:T(8,128)(2,1)} %get-tuple-element.260, s32[]{:T(128)S(6)} %copy.72, bf16[2,896,128]{2,1,0:T(8,128)(2,1)} %get-tuple-element.259), kind=kOutput, calls=%fused_computation.7.clone.1 | convolution fusion | flops 954203264 | bytes 15982592 | tf_op jit(solution)/shard_map/while/body/eval_jaxpr/dot_general | solution.py:54
  285.3 1.6 fusion.60
  286.9 8.8 %fusion.61 = f32[896]{0:T(1024)S(1)} fusion(f32[896,4096]{1,0:T(8,128)} %get-tuple-element.233, s32[4096]{0:T(1024)S(1)} %get-tuple-element.264, f32[896]{0:T(1024)S(1)} %max.23, s32[896]{0:T(1024)S(1)} %get-tuple-element.265), kind=kLoop, calls=%fused_computation.6.clone.1 | loop fusion | flops 18349184 | bytes 14707200 | tf_op jit(solution)/shard_map/while/body/eval_jaxpr/reduce_sum | solution.py:61
  295.7 0.5 fusion.62
  296.2 7.7 %fusion.63 = f32[896,128]{1,0:T(8,128)S(1)} fusion(f32[896,4096]{1,0:T(8,128)} %get-tuple-element.233, s32[4096]{0:T(1024)S(1)} %get-tuple-element.264, f32[896]{0:T(1024)S(1)} %add.169, f32[896]{0:T(1024)S(1)} %max.23, s32[896]{0:T(1024)S(1)} %get-tuple-element.265, bf16[2,4096,128]{2,1,0:T(8,128)(2,1)S(1)} %copy-done.7, s32[]{:T(128)S(6)} %copy.72), kind=kOutput, calls=%fused_computation.8.clone.1 | convolution fusion | flops 961544192 | bytes 16216068 | tf_op jit(solution)/shard_map/while/body/eval_jaxpr/dot_general | solution.py:64
  304.0 0.7 fusion.64
  304.7 0.2 copy.68
  304.8 0.1 copy-done.8
  305.0 0.8 copy-done.9
  305.8 8.0 %convolution_convert_fusion = bf16[896,5120]{1,0:T(8,128)(2,1)} fusion(bf16[896,256]{0,1:T(8,128)(2,1)} %bitcast.104, bf16[256,5120]{0,1:T(8,128)(2,1)} %all-gather.8.cloned.1.call-done), kind=kOutput, calls=%fused_computation.41 | convolution fusion | flops 2353397760 | bytes 12255232 | tf_op jit(solution)/shard_map/dot_general | solution.py:159
  313.9 0.6 copy-done.11
  314.5 0.1 select_reduce_fusion.2
  314.9 0.1 copy-done.5
  315.0 0.3 maximum_convert_fusion
  315.3 0.3 copy.56
  315.5 0.1 pad_maximum_fusion
  315.6 1.3 copy.57
  316.9 32.4 %gather_fusion = bf16[4096,2,256]{2,1,0:T(2,128)(2,1)} fusion(bf16[896,2,256]{2,1,0:T(2,128)(2,1)S(1)} %copy.57, s32[4096]{0:T(1024)S(1)} %broadcast_clamp_fusion), kind=kCustom, calls=%fused_computation | custom fusion | bytes 8404992 | tf_op jit(solution)/shard_map/jit(_take)/gather | solution.py:80
  349.3 12.7 %broadcast_select_fusion.1 = bf16[16,256,2,256]{3,2,1,0:T(2,128)(2,1)S(1)} fusion(pred[16,256]{1,0:T(8,128)(4,1)S(1)} %get-tuple-element.172, bf16[16,256,2,256]{3,2,1,0:T(2,128)(2,1)} %bitcast.98, pred[16,256]{1,0:T(8,128)(4,1)S(1)} %get-tuple-element.173), kind=kLoop, calls=%fused_computation.43 | loop fusion | flops 4194304 | bytes 8396800 | tf_op jit(solution)/shard_map/jit(_where)/select_n | solution.py:83
  362.0 109.6 %all_to_all.5 = bf16[16,256,2,256]{3,2,1,0:T(2,128)(2,1)} all-to-all(bf16[16,256,2,256]{3,2,1,0:T(2,128)(2,1)S(1)} %broadcast_select_fusion.1), channel_id=1, replica_groups=mesh['req'=16,'tp'=16] {'req'}, dimensions={0} | all-to-all | bytes 8388608 | tf_op jit(solution)/shard_map/all_to_all | solution.py:88
  471.6 1.3 fusion.35
  472.9 2.1 fusion.38
  475.1 9.2 %copy.79 = bf16[32,128,2,256]{3,2,1,0:T(2,128)(2,1)} copy(bf16[32,128,2,256]{3,2,1,0:T(2,128)(2,1)} %bitcast.99) | data formatting | bytes 8388608
  (64 shorter events, 0.9 us)
Async XLA Ops:
  7.2 83.5 %all-gather.6.cloned.1.call-start = ((), (), s32[]{:S(2)}) async-start(), calls=%async_computation.3 | async-start | bytes 8355840 | tf_op jit(solution)/shard_map/all_gather | solution.py:108
  7.9 191.0 %all-gather.4.cloned.1.call-start = ((), (), s32[]{:S(2)}) async-start(), calls=%async_computation.2 | async-start | bytes 9748480 | tf_op jit(solution)/shard_map/all_gather | solution.py:106
  8.6 297.1 %all-gather.8.cloned.1.call-start = ((), (), s32[]{:S(2)}) async-start(), calls=%async_computation.4 | async-start | bytes 2785280 | tf_op jit(solution)/shard_map/all_gather | solution.py:157
  9.4 462.2 %reduce-scatter.2.cloned.1.call-start = ((), (), s32[]{:S(2)}) async-start(), calls=%async_computation.5 | async-start | bytes 9748480 | tf_op jit(solution)/shard_map/reduce_scatter | solution.py:158
  34.2 6.5 %copy-start.12 = (s32[1,16]{1,0:T(1,128)S(1)}, s32[1,16]{1,0:T(1,128)}, u32[]{:S(2)}) copy-start(s32[1,16]{1,0:T(1,128)} %param.19) | copy-start | bytes 196
  34.2 6.9 %copy-start.15 = (s32[1,32]{1,0:T(1,128)S(1)}, s32[1,32]{1,0:T(1,128)}, u32[]{:S(2)}) copy-start(s32[1,32]{1,0:T(1,128)} %param.20) | copy-start | bytes 388
  212.1 32.6 %copy-start = (bf16[896,1,256]{0,2,1:T(8,128)(2,1)}, bf16[896,1,256]{0,2,1:T(8,128)(2,1)S(1)}, u32[]{:S(2)}) copy-start(bf16[896,1,256]{0,2,1:T(8,128)(2,1)S(1)} %slice.78) | copy-start | bytes 1376260
  244.6 1.6 copy-start.2
  244.6 1.6 copy-start.4
  257.2 9.3 %copy-start.7 = (bf16[2,4096,128]{2,1,0:T(8,128)(2,1)S(1)}, bf16[2,4096,128]{2,1,0:T(8,128)(2,1)}, u32[]{:S(2)}) copy-start(bf16[2,4096,128]{2,1,0:T(8,128)(2,1)} %get-tuple-element.262) | copy-start | bytes 6291460 | tf_op jit(solution)/shard_map/while
  274.2 1.0 copy-start.8
  275.3 0.8 copy-start.9
  286.9 9.3 %copy-start.7 = (bf16[2,4096,128]{2,1,0:T(8,128)(2,1)S(1)}, bf16[2,4096,128]{2,1,0:T(8,128)(2,1)}, u32[]{:S(2)}) copy-start(bf16[2,4096,128]{2,1,0:T(8,128)(2,1)} %get-tuple-element.262) | copy-start | bytes 6291460 | tf_op jit(solution)/shard_map/while
  304.0 1.0 copy-start.8
  305.0 0.8 copy-start.9
  313.8 0.7 copy-start.11
  313.8 0.7 copy-start.13
  313.8 0.7 copy-start.14
  313.8 1.0 copy-start.3
  313.8 1.2 copy-start.5
  313.8 1.7 copy-start.1
  362.0 110.9 %copy-start.6 = (bf16[56,5120]{1,0:T(8,128)(2,1)S(1)}, bf16[56,5120]{1,0:T(8,128)(2,1)}, u32[]{:S(2)}) copy-start(bf16[56,5120]{1,0:T(8,128)(2,1)} %param.12) | copy-start | bytes 1720324
  362.0 110.9 %copy-start.10 = (f32[5120]{0:T(1024)S(1)}, f32[5120]{0:T(1024)}, u32[]{:S(2)}) copy-start(f32[5120]{0:T(1024)} %param.16) | copy-start | bytes 61444
Sparse Core Ops, SparseCore 0:
  10.8 79.8 all-gather.5
  92.5 106.3 all-gather.3
  201.6 53.9 all-gather.7
  314.0 145.7 reduce-scatter.1
where the time goes:
time: 492 us; the launch traced here: 491 us
  waiting for transfers between devices  143 us (29%)
  blocking collectives  136 us (28%)
  local copies, waits for them, and re-layouts  95.2 us (19%)
  matrix products  58.7 us (12%)
  other arithmetic  43.9 us (9%)
  between operations  14 us (3%)
    all_to_all x1, blocking collectives, hand_over(): lax.all_to_all(outgoing, 'req', split_axis=0, concat_axis=0, tiled=True)  110 us
    all_gather x1, waiting for transfers between devices, body(): block_tokens = lax.all_gather(tokens, 'tp', axis=0, tiled=True)  97.4 us
    all_gather x1, waiting for transfers between devices, body(): row_piece = lax.all_gather(qkv_weight, 'req', axis=0, tiled=True)  43.6 us
    gather x1, local copies, waits for them, and re-layouts, build_send(): jnp.take(kv_new, source, axis=0)  32.4 us
    psum x1, blocking collectives, body(): global_sums = lax.psum(local_sums, 'tp')  26 us
    slice x1, local copies, waits for them, and re-layouts, body(): pool_cache[:, :, 1, :].reshape(pool_count * PAGE, heads_here, HEAD)  21.7 us
    reduce_sum x4, other arithmetic, attend_head(): row_total = jnp.sum(pool_exp, axis=1) + jnp.sum(block_exp, axis=1)  18.6 us
    dot_general x2, matrix products, attend_head(): jnp.dot(queries, pool_keys.T, preferred_element_type=jnp.float32)  18.5 us
  transfers between devices with their start and end apart: 4, of which 2 were waited for; matrix products, arithmetic and copies ran while one was open for 36% of the time, Pallas kernels for 0%

commit v1 on v0

--- a/solution.py
+++ b/solution.py
@@ -103,7 +103,9 @@
 ):
     local_width = qkv_weight.shape[2]
     heads_here = local_width // HEAD
-    block_tokens = lax.all_gather(tokens, "tp", axis=0, tiled=True)
+    block_tokens = jnp.concatenate(
+        lax.all_to_all(jnp.stack([tokens] * lax.axis_size("tp")), "tp", 0, 0), axis=0
+    )
     block_len = block_tokens.shape[0]
     row_piece = lax.all_gather(qkv_weight, "req", axis=0, tiled=True)
     flat_piece = row_piece.reshape(row_piece.shape[0], 3 * local_width)

time: 492 us -> 527 us (1.071)
  waiting for transfers between devices: 143 us -> 159 us
  starting transfers between devices: 0.15 us -> 10.4 us
    all_gather x1 -> x0, waiting for transfers between devices: 97.4 us -> none  [body(): block_tokens = lax.all_gather(tokens, 'tp', axis=0, tiled=True)]
    all_to_all x0 -> x1, waiting for transfers between devices: none -> 67 us  [body(): lax.all_to_all(jnp.stack([tokens] * lax.axis_size('tp')), 'tp', 0, 0)]
    all_gather x1, waiting for transfers between devices: 43.6 us -> 90.3 us  [body(): row_piece = lax.all_gather(qkv_weight, 'req', axis=0, tiled=True)]
    all_to_all x0 -> x1, starting transfers between devices: none -> 10.3 us  [body(): lax.all_to_all(jnp.stack([tokens] * lax.axis_size('tp')), 'tp', 0, 0)]
    another operation x1 -> x2, local copies, waits for them, and re-layouts: 0.08 us -> 5.84 us  [the longest x1 5.75 us: body(): jnp.stack([tokens] * lax.axis_size('tp'))]
    psum x1, blocking collectives: 26 us -> 31.7 us  [body(): global_sums = lax.psum(local_sums, 'tp')]
    unnamed x29 -> x33, local copies, waits for them, and re-layouts: 14.2 us -> 14.2 us
  transfers between devices with their start and end apart: 4 -> 4, of which waited for: 2 -> 2; matrix products, arithmetic and copies ran while one was open for 36% -> 34% of each run, Pallas kernels for 0% -> 0%
where the time goes in v1:
time: 527 us; the launch traced here: 526 us
  waiting for transfers between devices  159 us (30%)
  blocking collectives  141 us (27%)
  local copies, waits for them, and re-layouts  99.3 us (19%)
  matrix products  58.6 us (11%)
  other arithmetic  43.2 us (8%)
  between operations  14.1 us (3%)
  starting transfers between devices  10.4 us (2%)
    all_to_all x1, blocking collectives, hand_over(): lax.all_to_all(outgoing, 'req', split_axis=0, concat_axis=0, tiled=True)  110 us
    all_gather x1, waiting for transfers between devices, body(): row_piece = lax.all_gather(qkv_weight, 'req', axis=0, tiled=True)  90.3 us
    all_to_all x1, waiting for transfers between devices, body(): lax.all_to_all(jnp.stack([tokens] * lax.axis_size('tp')), 'tp', 0, 0)  67 us
    gather x1, local copies, waits for them, and re-layouts, build_send(): jnp.take(kv_new, source, axis=0)  32.4 us
    psum x1, blocking collectives, body(): global_sums = lax.psum(local_sums, 'tp')  31.7 us
    slice x1, local copies, waits for them, and re-layouts, body(): pool_cache[:, :, 1, :].reshape(pool_count * PAGE, heads_here, HEAD)  21.6 us
    reduce_sum x4, other arithmetic, attend_head(): row_total = jnp.sum(pool_exp, axis=1) + jnp.sum(block_exp, axis=1)  18.6 us
    dot_general x2, matrix products, attend_head(): jnp.dot(queries, pool_keys.T, preferred_element_type=jnp.float32)  18.5 us
  transfers between devices with their start and end apart: 4, of which 2 were waited for; matrix products, arithmetic and copies ran while one was open for 34% of the time, Pallas kernels for 0%

profile of v1, /device:TPU:1, one launch (start us, length us, event | category | flops | bytes accessed | tf_op | source)
XLA Modules:
  0.0 525.8 jit_solution(8540063974792696077)
XLA Ops:
  7.2 0.7 all-gather.3.cloned.1.call-update
  7.9 5.8 %stack.10 = bf16[16,56,5120]{2,1,0:T(8,128)(2,1)} broadcast(bf16[56,5120]{1,0:T(8,128)(2,1)} %param.12), dimensions={1,2} | broadcast | bytes 9748480 | tf_op jit(solution)/shard_map/stack | solution.py:107
  13.7 10.3 %all-to-all-start = ((bf16[16,56,5120]{2,1,0:T(8,128)(2,1)}), bf16[16,56,5120]{2,1,0:T(8,128)(2,1)}, u32[]{:S(2)}, u32[]{:S(2)}) async-start(bf16[16,56,5120]{2,1,0:T(8,128)(2,1)} %stack.10), calls=%async_computation | async-start | bytes 18350080 | tf_op jit(solution)/shard_map/all_to_all | solution.py:107
  24.0 0.7 all-gather.5.cloned.1.call-update
  24.8 0.1 copy.47
  24.9 0.1 reduce.3
  25.0 21.6 %slice_reduce_fusion = (bf16[32,128,256]{2,1,0:T(8,128)(2,1)}, bf16[32,128,256]{2,1,0:T(8,128)(2,1)}) fusion(bf16[32,128,2,256]{3,2,1,0:T(2,128)(2,1)} %param.17), kind=kLoop, calls=%fused_computation.44 | loop fusion | bytes 8388608 | tf_op jit(solution)/shard_map/slice | solution.py:145
  46.7 2.6 reshape.266
  49.3 4.0 reshape.265
  53.2 0.1 copy.52
  53.4 0.1 reduce.8
  53.5 0.1 convert_reduce_fusion.1
  53.6 0.1 select_reduce_fusion.1
  53.7 0.1 convert_reduce_fusion
  53.8 0.5 fusion.42
  54.5 1.7 multiply_cosine_fusion
  56.2 4.1 copy_bitcast_fusion
  60.3 90.3 %all-gather.3.cloned.1.call-done = bf16[5120,3,256]{2,0,1:T(8,128)(2,1)} async-done(((bf16[320,3,256]{2,0,1:T(8,128)(2,1)}), bf16[5120,3,256]{2,0,1:T(8,128)(2,1)}) %all-gather.3.cloned.1.call-update) | async-done | bytes 7864336 | tf_op jit(solution)/shard_map/all_gather | solution.py:110
  150.6 10.7 %copy.45 = bf16[5120,3,256]{0,2,1:T(8,128)(2,1)} copy(bf16[5120,3,256]{2,0,1:T(8,128)(2,1)} %all-gather.3.cloned.1.call-done) | data formatting | bytes 15728640 | tf_op jit(solution)/shard_map/all_gather | solution.py:110
  161.3 67.0 %all-to-all-done = bf16[16,56,5120]{2,1,0:T(8,128)(2,1)} async-done(((bf16[16,56,5120]{2,1,0:T(8,128)(2,1)}), bf16[16,56,5120]{2,1,0:T(8,128)(2,1)}, u32[]{:S(2)}, u32[]{:S(2)}) %all-to-all-start) | async-done | bytes 9175072 | tf_op jit(solution)/shard_map/all_to_all | solution.py:107
  228.3 12.0 %fusion.32 = f32[896,3,256]{0,2,1:T(8,128)S(1)} fusion(bf16[896,5120,1]{1,0,2:T(8,128)(2,1)} %bitcast.1, bf16[5120,3,256]{0,2,1:T(8,128)(2,1)} %copy.45), kind=kOutput, calls=%fused_computation.42 | convolution fusion | flops 7046430720 | bytes 19791872 | tf_op jit(solution)/shard_map/dot_general | solution.py:112
  240.3 1.1 multiply_reduce_fusion.1
  241.5 2.6 copy.49
  244.1 31.7 %psum.7 = f32[2,896]{1,0:T(2,128)S(1)} all-reduce(f32[2,896]{1,0:T(2,128)S(1)} %pad_maximum_fusion.1), channel_id=1, replica_groups=mesh['req'=16,'tp'=16] {'tp'}, use_global_device_ids=true, to_apply=%region_2.0 | all-reduce | flops 1792 | bytes 14336 | tf_op jit(solution)/shard_map/psum | solution.py:120
  275.8 1.2 copy.46
  277.1 1.8 multiply_multiply_fusion
  278.8 0.4 subtract_convert_fusion
  279.2 0.4 multiply_subtract_fusion
  279.7 0.3 copy.51
  280.0 1.0 maximum_bitcast_fusion
  281.0 0.3 fusion.48
  281.3 59.5 %while.12 = (s32[]{:T(128)}, bf16[2,896,128]{1,2,0:T(8,128)(2,1)}, bf16[2,896,128]{2,1,0:T(8,128)(2,1)}, bf16[2,4096,128]{2,1,0:T(8,128)(2,1)}, bf16[2,896,128]{...) while((s32[]{:T(128)}, bf16[2,896,128]{1,2,0:T(8,128)(2,1)}, ...), condition=%wide.region_14.15_spmd.clone.clone, body=%wide.region_9.14_spmd.clone.clone.sunk | while | flops 2354198784 | bytes 70941888 | solution.py:146
  281.3 9.2 %fusion.59 = (f32[896]{0:T(1024)S(1)}, f32[896,4096]{1,0:T(8,128)}) fusion(s32[4096]{0:T(1024)S(1)} %get-tuple-element.264, s32[896]{0:T(1024)S(1)} %get-tuple-element.265, bf16[2,4096,128]{2,1,0:T(8,128)(2,1)} %get-tuple-element.260, s32[]{:T(128)S(6)} %copy.72, bf16[2,896,128]{2,1,0:T(8,128)(2,1)} %get-tuple-element.259), kind=kOutput, calls=%fused_computation.7.clone.1 | convolution fusion | flops 954203264 | bytes 15982592 | tf_op jit(solution)/shard_map/while/body/eval_jaxpr/dot_general | solution.py:54
  290.5 1.6 fusion.60
  292.2 8.8 %fusion.61 = f32[896]{0:T(1024)S(1)} fusion(f32[896,4096]{1,0:T(8,128)} %get-tuple-element.233, s32[4096]{0:T(1024)S(1)} %get-tuple-element.264, f32[896]{0:T(1024)S(1)} %max.23, s32[896]{0:T(1024)S(1)} %get-tuple-element.265), kind=kLoop, calls=%fused_computation.6.clone.1 | loop fusion | flops 18349184 | bytes 14707200 | tf_op jit(solution)/shard_map/while/body/eval_jaxpr/reduce_sum | solution.py:61
  301.0 0.5 fusion.62
  301.5 7.7 %fusion.63 = f32[896,128]{1,0:T(8,128)S(1)} fusion(f32[896,4096]{1,0:T(8,128)} %get-tuple-element.233, s32[4096]{0:T(1024)S(1)} %get-tuple-element.264, f32[896]{0:T(1024)S(1)} %add.169, f32[896]{0:T(1024)S(1)} %max.23, s32[896]{0:T(1024)S(1)} %get-tuple-element.265, bf16[2,4096,128]{2,1,0:T(8,128)(2,1)S(1)} %copy-done.7, s32[]{:T(128)S(6)} %copy.72), kind=kOutput, calls=%fused_computation.8.clone.1 | convolution fusion | flops 961544192 | bytes 16216068 | tf_op jit(solution)/shard_map/while/body/eval_jaxpr/dot_general | solution.py:64
  309.2 0.7 fusion.64
  309.9 0.2 copy.68
  310.1 0.1 copy-done.8
  310.3 0.8 copy-done.9
  311.0 9.2 %fusion.59 = (f32[896]{0:T(1024)S(1)}, f32[896,4096]{1,0:T(8,128)}) fusion(s32[4096]{0:T(1024)S(1)} %get-tuple-element.264, s32[896]{0:T(1024)S(1)} %get-tuple-element.265, bf16[2,4096,128]{2,1,0:T(8,128)(2,1)} %get-tuple-element.260, s32[]{:T(128)S(6)} %copy.72, bf16[2,896,128]{2,1,0:T(8,128)(2,1)} %get-tuple-element.259), kind=kOutput, calls=%fused_computation.7.clone.1 | convolution fusion | flops 954203264 | bytes 15982592 | tf_op jit(solution)/shard_map/while/body/eval_jaxpr/dot_general | solution.py:54
  320.3 1.6 fusion.60
  321.9 8.8 %fusion.61 = f32[896]{0:T(1024)S(1)} fusion(f32[896,4096]{1,0:T(8,128)} %get-tuple-element.233, s32[4096]{0:T(1024)S(1)} %get-tuple-element.264, f32[896]{0:T(1024)S(1)} %max.23, s32[896]{0:T(1024)S(1)} %get-tuple-element.265), kind=kLoop, calls=%fused_computation.6.clone.1 | loop fusion | flops 18349184 | bytes 14707200 | tf_op jit(solution)/shard_map/while/body/eval_jaxpr/reduce_sum | solution.py:61
  330.7 0.5 fusion.62
  331.2 7.7 %fusion.63 = f32[896,128]{1,0:T(8,128)S(1)} fusion(f32[896,4096]{1,0:T(8,128)} %get-tuple-element.233, s32[4096]{0:T(1024)S(1)} %get-tuple-element.264, f32[896]{0:T(1024)S(1)} %add.169, f32[896]{0:T(1024)S(1)} %max.23, s32[896]{0:T(1024)S(1)} %get-tuple-element.265, bf16[2,4096,128]{2,1,0:T(8,128)(2,1)S(1)} %copy-done.7, s32[]{:T(128)S(6)} %copy.72), kind=kOutput, calls=%fused_computation.8.clone.1 | convolution fusion | flops 961544192 | bytes 16216068 | tf_op jit(solution)/shard_map/while/body/eval_jaxpr/dot_general | solution.py:64
  339.0 0.7 fusion.64
  339.7 0.2 copy.68
  339.8 0.1 copy-done.8
  340.0 0.8 copy-done.9
  340.8 8.0 %convolution_convert_fusion = bf16[896,5120]{1,0:T(8,128)(2,1)} fusion(bf16[896,256]{0,1:T(8,128)(2,1)} %bitcast.105, bf16[256,5120]{0,1:T(8,128)(2,1)} %all-gather.5.cloned.1.call-done), kind=kOutput, calls=%fused_computation.39 | convolution fusion | flops 2353397760 | bytes 12255232 | tf_op jit(solution)/shard_map/dot_general | solution.py:161
  348.8 0.6 copy-done.12
  349.5 0.1 select_reduce_fusion.2
  349.8 0.1 copy-done.5
  350.0 0.3 maximum_convert_fusion
  350.2 0.3 copy.56
  350.5 0.1 pad_maximum_fusion
  350.6 1.3 copy.57
  351.9 32.4 %gather_fusion = bf16[4096,2,256]{2,1,0:T(2,128)(2,1)} fusion(bf16[896,2,256]{2,1,0:T(2,128)(2,1)S(1)} %copy.57, s32[4096]{0:T(1024)S(1)} %broadcast_clamp_fusion), kind=kCustom, calls=%fused_computation | custom fusion | bytes 8404992 | tf_op jit(solution)/shard_map/jit(_take)/gather | solution.py:80
  384.3 12.7 %broadcast_select_fusion.1 = bf16[16,256,2,256]{3,2,1,0:T(2,128)(2,1)S(1)} fusion(pred[16,256]{1,0:T(8,128)(4,1)S(1)} %get-tuple-element.172, bf16[16,256,2,256]{3,2,1,0:T(2,128)(2,1)} %bitcast.99, pred[16,256]{1,0:T(8,128)(4,1)S(1)} %get-tuple-element.173), kind=kLoop, calls=%fused_computation.41 | loop fusion | flops 4194304 | bytes 8396800 | tf_op jit(solution)/shard_map/jit(_where)/select_n | solution.py:83
  397.0 109.6 %all_to_all.10 = bf16[16,256,2,256]{3,2,1,0:T(2,128)(2,1)} all-to-all(bf16[16,256,2,256]{3,2,1,0:T(2,128)(2,1)S(1)} %broadcast_select_fusion.1), channel_id=1, replica_groups=mesh['req'=16,'tp'=16] {'req'}, dimensions={0} | all-to-all | bytes 8388608 | tf_op jit(solution)/shard_map/all_to_all | solution.py:88
  506.6 1.3 fusion.34
  507.9 2.1 fusion.37
  510.1 9.2 %copy.79 = bf16[32,128,2,256]{3,2,1,0:T(2,128)(2,1)} copy(bf16[32,128,2,256]{3,2,1,0:T(2,128)(2,1)} %bitcast.100) | data formatting | bytes 8388608
  (68 shorter events, 0.9 us)
Async XLA Ops:
  7.2 143.5 %all-gather.3.cloned.1.call-start = ((), (), s32[]{:S(2)}) async-start(), calls=%async_computation.3 | async-start | bytes 8355840 | tf_op jit(solution)/shard_map/all_gather | solution.py:110
  13.7 11.1 %copy-start.11 = (s32[1,16]{1,0:T(1,128)S(1)}, s32[1,16]{1,0:T(1,128)}, u32[]{:S(2)}) copy-start(s32[1,16]{1,0:T(1,128)} %param.18) | copy-start | bytes 196
  13.7 214.6 %all-to-all-start = ((bf16[16,56,5120]{2,1,0:T(8,128)(2,1)}), bf16[16,56,5120]{2,1,0:T(8,128)(2,1)}, u32[]{:S(2)}, u32[]{:S(2)}) async-start(bf16[16,56,5120]{2,1,0:T(8,128)(2,1)} %stack.10), calls=%async_computation | async-start | bytes 18350080 | tf_op jit(solution)/shard_map/all_to_all | solution.py:107
  24.0 316.8 %all-gather.5.cloned.1.call-start = ((), (), s32[]{:S(2)}) async-start(), calls=%async_computation.4 | async-start | bytes 2785280 | tf_op jit(solution)/shard_map/all_gather | solution.py:159
  24.7 481.9 %reduce-scatter.2.cloned.1.call-start = ((), (), s32[]{:S(2)}) async-start(), calls=%async_computation.5 | async-start | bytes 9748480 | tf_op jit(solution)/shard_map/reduce_scatter | solution.py:160
  46.7 6.6 %copy-start.13 = (s32[1,16]{1,0:T(1,128)S(1)}, s32[1,16]{1,0:T(1,128)}, u32[]{:S(2)}) copy-start(s32[1,16]{1,0:T(1,128)} %param.19) | copy-start | bytes 196
  46.7 6.9 %copy-start.17 = (s32[1,32]{1,0:T(1,128)S(1)}, s32[1,32]{1,0:T(1,128)}, u32[]{:S(2)}) copy-start(s32[1,32]{1,0:T(1,128)} %param.20) | copy-start | bytes 388
  46.7 7.7 %copy-start.15 = (f32[2,256]{1,0:T(2,128)S(1)}, f32[2,256]{1,0:T(2,128)}, u32[]{:S(2)}) copy-start(f32[2,256]{1,0:T(2,128)} %param.15) | copy-start | bytes 6148
  241.5 38.2 %copy-start = (bf16[896,1,256]{0,2,1:T(8,128)(2,1)}, bf16[896,1,256]{0,2,1:T(8,128)(2,1)S(1)}, u32[]{:S(2)}) copy-start(bf16[896,1,256]{0,2,1:T(8,128)(2,1)S(1)} %slice.78) | copy-start | bytes 1376260
  279.7 1.6 copy-start.2
  279.7 1.6 copy-start.4
  292.2 9.3 %copy-start.7 = (bf16[2,4096,128]{2,1,0:T(8,128)(2,1)S(1)}, bf16[2,4096,128]{2,1,0:T(8,128)(2,1)}, u32[]{:S(2)}) copy-start(bf16[2,4096,128]{2,1,0:T(8,128)(2,1)} %get-tuple-element.262) | copy-start | bytes 6291460 | tf_op jit(solution)/shard_map/while
  309.2 1.0 copy-start.8
  310.3 0.8 copy-start.9
  321.9 9.3 %copy-start.7 = (bf16[2,4096,128]{2,1,0:T(8,128)(2,1)S(1)}, bf16[2,4096,128]{2,1,0:T(8,128)(2,1)}, u32[]{:S(2)}) copy-start(bf16[2,4096,128]{2,1,0:T(8,128)(2,1)} %get-tuple-element.262) | copy-start | bytes 6291460 | tf_op jit(solution)/shard_map/while
  338.9 1.0 copy-start.8
  340.0 0.8 copy-start.9
  348.8 0.7 copy-start.12
  348.8 0.7 copy-start.14
  348.8 0.7 copy-start.16
  348.8 1.0 copy-start.3
  348.8 1.2 copy-start.5
  348.8 1.7 copy-start.1
  397.0 111.0 %copy-start.6 = (bf16[56,5120]{1,0:T(8,128)(2,1)S(1)}, bf16[56,5120]{1,0:T(8,128)(2,1)}, u32[]{:S(2)}) copy-start(bf16[56,5120]{1,0:T(8,128)(2,1)} %param.12) | copy-start | bytes 1720324
  397.0 111.0 %copy-start.10 = (f32[5120]{0:T(1024)S(1)}, f32[5120]{0:T(1024)}, u32[]{:S(2)}) copy-start(f32[5120]{0:T(1024)} %param.16) | copy-start | bytes 61444
Sparse Core Ops, SparseCore 0:
  10.8 139.8 all-gather.2
  153.3 77.5 all-gather.4
  349.0 145.7 reduce-scatter.1
